TPU v7x, 32 devices: a whole 2x2x4 slice. The times are simulated.
32 devices in a mesh: width: 4 (over y, core), hidden: 8 (over z, x).
Axes of the slice: x: 2, y: 2, z: 4, core: 2. Of those that a mesh axis runs over, the one named last changes fastest.
Arguments:
- tokens: bfloat16 [1152, 5120], P(None, 'width'), may hold values from -6 to 6
- cotangent: bfloat16 [1152, 5120], P(None, 'width'), may hold values from -6 to 6
- w_up: bfloat16 [5120, 13824], P('width', 'hidden'), may hold values from -0.078125 to 0.078125
- bias_up: float32 [13824], P('hidden'), may hold values from -3 to 3
- w_down: bfloat16 [13824, 5120], P('hidden', 'width'), may hold values from -0.0546875 to 0.0546875
- mod_table: float32 [32, 3, 5120], P(None, None, 'width'), may hold values from -3 to 3
- seg_ids: int32 [1152], replicated, may hold values from 0 to 15, never falling along the last dimension, each value on 1 to 144 neighbouring positions
- step_ids: int32 [16], replicated, may hold values from 0 to 31
Outputs:
- grad_x: bfloat16 [1152, 5120], P(None, 'width')
- grad_up: float32 [5120, 13824], P('width', 'hidden')
- grad_down: float32 [13824, 5120], P('hidden', 'width')
- grad_bias: float32 [13824], P('hidden')
- grad_table: float32 [32, 3, 5120], P(None, None, 'width')
Inputs may be any that keep to these rules, and one draw needn't show every extreme that they name: `seg_ids`: request numbers never fall along the tokens and every request holds at least one token.
All inputs are finite; a program needn't handle non-finite values.
Results may differ from a plain program's by a relative error of at most 0.0063.
Values may be sent and summed in bfloat16 or wider, within the bound.
No kernel may reach another device: no remote copies, remote signals or barrier semaphores. Data moves between devices by JAX's collectives and lax.ppermute only.
A program may use at most 128 MiB of HBM per device.

v0:
```python
import jax
import jax.numpy as jnp
from jax import lax
from jax.sharding import PartitionSpec as P

D = 5120


def gelu_tanh(value):
    return jax.nn.gelu(value, approximate=True)


def norm_back(d_norm, x_hat, mod_gain, inv_std, cotangent):
    d_hat = d_norm * mod_gain
    feature_sums = lax.psum((jnp.sum(d_hat, 1), jnp.sum(d_hat * x_hat, 1)), "width")
    mean_one = feature_sums[0] / D
    mean_two = feature_sums[1] / D
    grad_rows = cotangent.astype(jnp.float32) + inv_std[:, None] * (
        d_hat - mean_one[:, None] - x_hat * mean_two[:, None]
    )
    return grad_rows.astype(jnp.bfloat16)


def per_device(tokens, cotangent, w_up, bias_up, w_down, mod_table, seg_ids, step_ids):
    highest = lax.Precision.HIGHEST
    req_count = step_ids.shape[0]
    table_rows = mod_table.shape[0]
    req_of = (seg_ids[:, None] == jnp.arange(req_count)[None, :]).astype(jnp.float32)
    step_of = (step_ids[:, None] == jnp.arange(table_rows)[None, :]).astype(jnp.float32)
    req_mod = jnp.einsum("rk,kcd->rcd", step_of, mod_table, precision=highest)
    shift_tok = jnp.dot(req_of, req_mod[:, 0], precision=highest)
    scale_tok = jnp.dot(req_of, req_mod[:, 1], precision=highest)
    gate_tok = jnp.dot(req_of, req_mod[:, 2], precision=highest)
    x_full = tokens.astype(jnp.float32)
    moment_one, moment_two = lax.psum((jnp.sum(x_full, 1), jnp.sum(x_full * x_full, 1)), "width")
    tok_mean = moment_one / D
    tok_var = moment_two / D - tok_mean * tok_mean
    inv_std = lax.rsqrt(tok_var + 1e-06)
    x_hat = (x_full - tok_mean[:, None]) * inv_std[:, None]
    mod_gain = 1.0 + scale_tok
    normed = (x_hat * mod_gain + shift_tok).astype(jnp.bfloat16)
    up_part = jnp.dot(normed, w_up, preferred_element_type=jnp.float32)
    pre_share = lax.psum_scatter(up_part, "width", scatter_dimension=0, tiled=True) + bias_up
    act_share = gelu_tanh(pre_share).astype(jnp.bfloat16)
    hidden_act = lax.all_gather(act_share, "width", axis=0, tiled=True)
    y_part = jnp.dot(hidden_act, w_down, preferred_element_type=jnp.float32)
    gate_part = jnp.dot(req_of.T, cotangent.astype(jnp.float32) * y_part, precision=highest)
    d_out = (cotangent.astype(jnp.float32) * gate_tok).astype(jnp.bfloat16)
    down_part = jnp.dot(d_out, w_down.T, preferred_element_type=jnp.float32)
    act_grad = lax.psum_scatter(down_part, "width", scatter_dimension=0, tiled=True)
    _, pull = jax.vjp(gelu_tanh, pre_share)
    pre_grad = pull(act_grad)[0]
    grad_bias = lax.psum(jnp.sum(pre_grad, 0), "width")
    d_pre_b = lax.all_gather(pre_grad.astype(jnp.bfloat16), "width", axis=0, tiled=True)
    grad_down = jnp.dot(hidden_act.T, d_out, preferred_element_type=jnp.float32)
    grad_up = jnp.dot(normed.T, d_pre_b, preferred_element_type=jnp.float32)
    d_part = jnp.dot(d_pre_b, w_up.T, preferred_element_type=jnp.float32)
    shift_part = jnp.dot(req_of.T, d_part, precision=highest)
    scale_part = jnp.dot(req_of.T, d_part * x_hat, precision=highest)
    req_grads = lax.psum(jnp.stack([shift_part, scale_part, gate_part], 1), "hidden")
    grad_table = jnp.einsum("rk,rcd->kcd", step_of, req_grads, precision=highest)
    d_norm = lax.psum(d_part, "hidden")
    grad_x = norm_back(d_norm, x_hat, mod_gain, inv_std, cotangent)
    return (grad_x, grad_up, grad_down, grad_bias, grad_table)


def solution(mesh):
    placed = (
        P(None, "width"),
        P(None, "width"),
        P("width", "hidden"),
        P("hidden"),
        P("hidden", "width"),
        P(None, None, "width"),
        P(),
        P(),
    )
    return jax.shard_map(
        per_device,
        mesh=mesh,
        in_specs=placed,
        out_specs=(
            P(None, "width"),
            P("width", "hidden"),
            P("hidden", "width"),
            P("hidden"),
            P(None, None, "width"),
        ),
        check_vma=False,
    )
```

profile of v0, /device:TPU:0, one launch (start us, length us, event | category | flops | bytes accessed | tf_op | source)
XLA Modules:
  0.0 515.7 jit_solution(15026594114937513184)
XLA Ops:
  7.2 0.0 copy-start
  7.2 0.0 copy-start.2
  7.2 0.0 copy-start.9
  7.2 0.0 reduce-scatter.5.cloned.1.call-start
  7.3 2.9 fusion.3
  10.1 12.7 %all-reduce.2 = (f32[1152]{0:T(1024)S(1)}, f32[1152]{0:T(1024)S(1)}) all-reduce(f32[1152]{0:T(1024)S(1)} %get-tuple-element.8, f32[1152]{0:T(1024)S(1)} %get-tuple-element.7), channel_id=1, replica_groups=mesh['width'=4,'hidden'=8] {'width'}, use_global_device_ids=true, to_apply=%region_3.0 | all-reduce | flops 2304 | bytes 18432 | tf_op jit(solution)/shard_map/psum | solution.py:35
  22.9 0.0 copy-done
  22.9 1.0 fusion.34
  23.9 0.0 copy-start.8
  23.9 0.0 slice-start
  23.9 3.4 convolution_add_fusion.1
  27.2 0.0 copy-start.3
  27.3 0.0 copy-done.8
  27.3 2.5 copy-done.3
  29.8 0.0 copy-done.2
  29.8 0.0 copy-done.9
  29.8 0.0 slice-start.1
  29.8 3.7 fusion.1
  33.5 0.0 copy-start.5
  33.6 1.6 copy-done.5
  35.1 0.0 slice-done
  35.1 0.0 slice-done.1
  35.2 7.7 %fusion.42 = f32[1152,1728]{1,0:T(8,128)} fusion(bf16[1152,1280]{1,0:T(8,128)(2,1)S(1)} %fusion.1, bf16[1280,1728]{0,1:T(8,128)(2,1)S(1)} %bitcast.36), kind=kOutput, calls=%fused_computation.59 | convolution fusion | flops 5096079360 | bytes 15335424 | tf_op jit(solution)/shard_map/dot_general | solution.py:42
  42.9 0.0 reduce-scatter.5.cloned.1.call-update
  42.9 0.0 reduce-scatter.3.cloned.1.call-start
  43.0 4.5 fusion
  47.4 0.0 copy-start.6
  47.5 1.7 copy-done.6
  49.1 10.2 %fusion.41 = f32[1152,1728]{1,0:T(8,128)} fusion(bf16[1152,1280]{1,0:T(8,128)(2,1)S(1)} %fusion, bf16[1728,1280]{1,0:T(8,128)(2,1)} %param.12), kind=kOutput, calls=%fused_computation.58 | convolution fusion | flops 5096079360 | bytes 15335424 | tf_op jit(solution)/shard_map/dot_general | solution.py:49
  59.4 0.0 reduce-scatter.3.cloned.1.call-update
  59.4 0.2 all-gather.3.cloned.1.call-start
  59.6 54.3 %reduce-scatter.5.cloned.1.call-done = f32[288,1728]{1,0:T(8,128)} async-done(((f32[1152,1728]{1,0:T(8,128)}), f32[288,1728]{1,0:T(8,128)}) %reduce-scatter.5.cloned.1.call-update) | async-done | bytes 1990672 | tf_op jit(solution)/shard_map/reduce_scatter | solution.py:43
  113.9 73.9 %reduce-scatter.3.cloned.1.call-done = f32[288,1728]{1,0:T(8,128)} async-done(((f32[1152,1728]{1,0:T(8,128)}), f32[288,1728]{1,0:T(8,128)}) %reduce-scatter.3.cloned.1.call-update) | async-done | bytes 1990672 | tf_op jit(solution)/shard_map/reduce_scatter | solution.py:50
  187.8 0.0 copy-done.11
  187.8 5.1 fusion.39
  192.9 0.0 all-gather.3.cloned.1.call-update
  193.0 0.0 all-gather.5.cloned.1.call-start
  193.0 0.5 all-gather.5.cloned.1.call-update
  193.5 0.0 all-reduce.5.cloned.1.call-start
  193.6 33.6 %all-gather.3.cloned.1.call-done = bf16[1152,1728]{1,0:T(8,128)(2,1)} async-done(((bf16[288,1728]{1,0:T(8,128)(2,1)}), bf16[1152,1728]{1,0:T(8,128)(2,1)}) %all-gather.3.cloned.1.call-update) | async-done | bytes 3981328 | tf_op jit(solution)/shard_map/all_gather | solution.py:54
  227.2 8.6 %fusion.43 = f32[1152,1280]{1,0:T(8,128)S(1)} fusion(bf16[1152,1728]{1,0:T(8,128)(2,1)} %all-gather.3.cloned.1.call-done, bf16[1280,1728]{0,1:T(8,128)(2,1)} %param.10), kind=kOutput, calls=%fused_computation.60 | convolution fusion | flops 5096079360 | bytes 14303232 | tf_op jit(solution)/shard_map/dot_general | solution.py:57
  235.8 0.0 copy-start.4
  235.8 2.1 convolution_bitcast_fusion.1
  237.9 0.8 copy-done.4
  238.7 2.8 fusion.16
  241.5 21.8 %all-gather.5.cloned.1.call-done = bf16[1152,1728]{1,0:T(8,128)(2,1)} async-done(((bf16[288,1728]{1,0:T(8,128)(2,1)}), bf16[1152,1728]{1,0:T(8,128)(2,1)}) %all-gather.5.cloned.1.call-update) | async-done | bytes 3981328 | tf_op jit(solution)/shard_map/all_gather | solution.py:45
  263.3 9.0 %convolution_multiply_fusion = f32[1152,1280]{1,0:T(8,128)S(1)} fusion(bf16[1152,1728]{1,0:T(8,128)(2,1)} %all-gather.5.cloned.1.call-done, bf16[1728,1280]{1,0:T(8,128)(2,1)} %param.12, bf16[1152,1280]{1,0:T(8,128)(2,1)} %param.9), kind=kOutput, calls=%fused_computation | convolution fusion | flops 5099028480 | bytes 17252352 | tf_op jit(solution)/shard_map/dot_general | solution.py:46
  272.4 2.1 convolution_bitcast_fusion
  274.5 0.7 pad_maximum_fusion
  275.2 0.0 all-reduce.5.cloned.1.call-update
  275.3 0.0 copy-start.7
  275.3 0.0 copy-start.13
  275.3 11.3 %fusion.44 = f32[1280,1728]{0,1:T(8,128)} fusion(bf16[1152,1280]{1,0:T(8,128)(2,1)} %copy-done.5, bf16[1152,1728]{1,0:T(8,128)(2,1)} %all-gather.3.cloned.1.call-done), kind=kOutput, calls=%fused_computation.61 | convolution fusion | flops 5096079360 | bytes 15777792 | tf_op jit(solution)/shard_map/dot_general | solution.py:56
  286.5 0.0 copy-done.7
  286.5 0.0 copy-done.13
  286.5 8.6 %fusion.45 = f32[1728,1280]{1,0:T(8,128)} fusion(bf16[1152,1728]{1,0:T(8,128)(2,1)S(1)} %copy-done.13, bf16[1152,1280]{1,0:T(8,128)(2,1)S(1)} %copy-done.7), kind=kOutput, calls=%fused_computation.62 | convolution fusion | flops 5096079360 | bytes 15777792 | tf_op jit(solution)/shard_map/dot_general | solution.py:55
  295.1 187.8 %all-reduce.5.cloned.1.call-done = (f32[1152,1280]{1,0:T(8,128)}, f32[16,3,1280]{2,0,1:T(8,128)}) async-done(((f32[1152,1280]{1,0:T(8,128)}, f32[16,3,1280]{2,0,1:T(8,128)}), (f32[1152,1280]{1,0:T(8,128)}, f32[16,3,1280]{2,0,1:T(8,128)})) %all-reduce.5.cloned.1.call-update) | async-done | bytes 6144016 | tf_op jit(solution)/shard_map/psum | solution.py:62
  482.9 8.0 %fusion.38 = (f32[1152]{0:T(1024)S(1)}, f32[1152]{0:T(1024)S(1)}, f32[1152,1280]{1,0:T(8,128)}) fusion(f32[1152]{0:T(1024)S(1)} %get-tuple-element.21, f32[1152]{0:T(1024)S(1)} %get-tuple-element.20, bf16[1152,1280]{1,0:T(8,128)(2,1)S(1)} %copy-done.2, f32[1152,1280]{1,0:T(8,128)} %get-tuple-element.9, f32[1152,1280]{1,0:T(8,128)} %copy-done.3), kind=kLoop, calls=%fused_computation.56 | loop fusion | flops 10319616 | bytes 20662272 | tf_op jit(solution)/shard_map/reduce_sum | solution.py:15
  490.8 0.0 copy-done.10
  490.8 0.0 copy-done.12
  490.8 1.3 fusion.32
  492.1 11.2 %all-reduce.1 = (f32[1152]{0:T(1024)S(1)}, f32[1152]{0:T(1024)S(1)}, f32[1728]{0:T(1024)}) all-reduce(f32[1152]{0:T(1024)S(1)} %get-tuple-element.6, f32[1152]{0:T(1024)S(1)} %get-tuple-element.5, f32[1728]{0:T(1024)S(1)} %get-tuple-element.16), channel_id=1, replica_groups=mesh['width'=4,'hidden'=8] {'width'}, use_global_device_ids=true, to_apply=%region_10.0 | all-reduce | flops 4032 | bytes 32256 | tf_op jit(solution)/shard_map/psum | solution.py:15
  503.3 5.9 %fusion.2 = bf16[1152,1280]{1,0:T(8,128)(2,1)} fusion(bf16[1152,1280]{1,0:T(8,128)(2,1)} %param.9, bf16[1152,1280]{1,0:T(8,128)(2,1)S(1)} %copy-done.2, f32[1152,1280]{1,0:T(8,128)} %get-tuple-element.18, f32[1152]{0:T(1024)S(1)} %get-tuple-element.22, f32[1152]{0:T(1024)S(1)} %get-tuple-element.23, f32[1152]{0:T(1024)S(1)} %get-tuple-element.20, ...), kind=kLoop, calls=%fused_computation.10 | loop fusion | flops 14745600 | bytes 14764032 | tf_op jit(solution)/shard_map/convert_element_type | solution.py:21
  509.1 0.0 copy-done.1
  (7 shorter events, 0.0 us)
Async XLA Ops:
  7.2 15.7 %copy-start = (f32[32,3,1280]{2,0,1:T(8,128)S(1)}, f32[32,3,1280]{2,0,1:T(8,128)}, u32[]{:S(2)}) copy-start(f32[32,3,1280]{2,0,1:T(8,128)} %param.13) | copy-start | bytes 1474564
  7.2 22.6 %copy-start.2 = (bf16[1152,1280]{1,0:T(8,128)(2,1)S(1)}, bf16[1152,1280]{1,0:T(8,128)(2,1)}, u32[]{:S(2)}) copy-start(bf16[1152,1280]{1,0:T(8,128)(2,1)} %param.8) | copy-start | bytes 8847364
  7.2 22.6 %copy-start.9 = (s32[1152]{0:T(1024)S(1)}, s32[1152]{0:T(1024)}, u32[]{:S(2)}) copy-start(s32[1152]{0:T(1024)} %param.14) | copy-start | bytes 13828
  7.2 106.7 %reduce-scatter.5.cloned.1.call-start = ((), (), s32[]{:S(2)}) async-start(), calls=%async_computation.3 | async-start | bytes 10321920 | tf_op jit(solution)/shard_map/reduce_scatter | solution.py:43
  23.9 3.4 copy-start.8
  23.9 11.3 %slice-start = ((s8[4423680]{0:T(1024)(128)(4,1)}), s8[4194304]{0:T(1024)(128)(4,1)S(1)}, s32[]{:S(2)}) async-start(s8[4423680]{0:T(1024)(128)(4,1)} %bitcast.35), calls=%async_computation.7 | async-start | bytes 8388608
  27.2 2.5 copy-start.3
  29.8 5.4 %slice-start.1 = ((s8[4423680]{0:T(1024)(128)(4,1)}), s8[229376]{0:T(1024)(128)(4,1)S(1)}, s32[]{:S(2)}) async-start(s8[4423680]{0:T(1024)(128)(4,1)} %bitcast.35), calls=%async_computation.8 | async-start | bytes 458752
  33.5 1.6 copy-start.5
  42.9 144.9 %reduce-scatter.3.cloned.1.call-start = ((), (), s32[]{:S(2)}) async-start(), calls=%async_computation.2 | async-start | bytes 10321920 | tf_op jit(solution)/shard_map/reduce_scatter | solution.py:50
  47.4 1.7 copy-start.6
  59.4 128.5 %copy-start.11 = (f32[1728]{0:T(1024)S(1)}, f32[1728]{0:T(1024)}, u32[]{:S(2)}) copy-start(f32[1728]{0:T(1024)} %param.11) | copy-start | bytes 20740
  59.4 167.8 %all-gather.3.cloned.1.call-start = ((), (), s32[]{:S(2)}) async-start(), calls=%async_computation.4 | async-start | bytes 5160960 | tf_op jit(solution)/shard_map/all_gather | solution.py:54
  193.0 70.4 %all-gather.5.cloned.1.call-start = ((), (), s32[]{:S(2)}) async-start(), calls=%async_computation.5 | async-start | bytes 5160960 | tf_op jit(solution)/shard_map/all_gather | solution.py:45
  193.5 289.3 %all-reduce.5.cloned.1.call-start = ((), (), s32[]{:S(2)}) async-start(), calls=%async_computation.6 | async-start | bytes 12288000 | tf_op jit(solution)/shard_map/psum | solution.py:62
  235.8 2.9 copy-start.4
  275.3 11.3 %copy-start.7 = (bf16[1152,1280]{1,0:T(8,128)(2,1)S(1)}, bf16[1152,1280]{1,0:T(8,128)(2,1)}, u32[]{:S(2)}) copy-start(bf16[1152,1280]{1,0:T(8,128)(2,1)} %copy-done.6) | copy-start | bytes 8847364
  275.3 11.3 %copy-start.13 = (bf16[1152,1728]{1,0:T(8,128)(2,1)S(1)}, bf16[1152,1728]{1,0:T(8,128)(2,1)}, u32[]{:S(2)}) copy-start(bf16[1152,1728]{1,0:T(8,128)(2,1)} %all-gather.5.cloned.1.call-done) | copy-start | bytes 11943940
  482.9 8.0 %copy-start.10 = (f32[16,3,1280]{2,0,1:T(8,128)S(1)}, f32[16,3,1280]{2,0,1:T(8,128)}, u32[]{:S(2)}) copy-start(f32[16,3,1280]{2,0,1:T(8,128)} %get-tuple-element.10) | copy-start | bytes 737284
  482.9 8.0 %copy-start.12 = (s32[16]{0:T(128)S(1)}, s32[16]{0:T(128)}, u32[]{:S(2)}) copy-start(s32[16]{0:T(128)} %param.15) | copy-start | bytes 196
  503.3 5.9 %copy-start.1 = (f32[32,3,1280]{2,0,1:T(8,128)S(1)}, f32[32,3,1280]{2,0,1:T(8,128)}, u32[]{:S(2)}) copy-start(f32[32,3,1280]{2,0,1:T(8,128)} %param.13) | copy-start | bytes 1474564
Sparse Core Ops, SparseCore 0:
  43.0 70.8 reduce-scatter.4
  117.2 70.6 reduce-scatter.2
  193.1 34.0 all-gather.2
  229.2 34.0 all-gather.4
  275.4 207.4 all-reduce.4
where the time goes:
time: 516 us
  waiting for transfers between devices  372 us (72%)
  matrix products  76.3 us (15%)
  blocking collectives  23.9 us (5%)
  other arithmetic  22.6 us (4%)
  between operations  13.9 us (3%)
  local copies, waits for them, and re-layouts  6.61 us (1%)
    psum x1, waiting for transfers between devices, per_device(): d_norm = lax.psum(d_part, 'hidden')  188 us
    reduce_scatter x1, waiting for transfers between devices, per_device(): lax.psum_scatter(down_part, 'width', scatter_dimension=0, tiled=True)  73.9 us
    reduce_scatter x1, waiting for transfers between devices, per_device(): lax.psum_scatter(up_part, 'width', scatter_dimension=0, tiled=True)  54.3 us
    all_gather x1, waiting for transfers between devices, per_device(): lax.all_gather(pre_grad.astype(jnp.bfloat16), 'width', axis=0, tiled=True)  33.6 us
    all_gather x1, waiting for transfers between devices, per_device(): hidden_act = lax.all_gather(act_share, 'width', axis=0, tiled=True)  21.8 us
    psum x1, blocking collectives, per_device(): lax.psum((jnp.sum(x_full, 1), jnp.sum(x_full * x_full, 1)), 'width')  12.7 us
    dot_general x1, matrix products, per_device(): grad_up = jnp.dot(normed.T, d_pre_b, preferred_element_type=jnp.float32)  11.3 us
    psum x1, blocking collectives, norm_back(): lax.psum((jnp.sum(d_hat, 1), jnp.sum(d_hat * x_hat, 1)), 'width')  11.2 us
  transfers between devices with their start and end apart: 5, of which 5 were waited for; matrix products, arithmetic and copies ran while one was open for 9% of the time, Pallas kernels for 0%

commit v1 on v0

--- a/solution.py
+++ b/solution.py
@@ -4,6 +4,15 @@
 from jax.sharding import PartitionSpec as P
 
 D = 5120
+
+
+def doubling_sum(x, axis):
+    peers = lax.axis_size(axis)
+    summed, far = (x, 1)
+    while far < peers:
+        summed = summed + lax.ppermute(summed, axis, [(i, i ^ far) for i in range(peers)])
+        far = 2 * far
+    return summed
 
 
 def gelu_tanh(value):
@@ -59,7 +68,7 @@
     scale_part = jnp.dot(req_of.T, d_part * x_hat, precision=highest)
     req_grads = lax.psum(jnp.stack([shift_part, scale_part, gate_part], 1), "hidden")
     grad_table = jnp.einsum("rk,rcd->kcd", step_of, req_grads, precision=highest)
-    d_norm = lax.psum(d_part, "hidden")
+    d_norm = doubling_sum(d_part, "hidden")
     grad_x = norm_back(d_norm, x_hat, mod_gain, inv_std, cotangent)
     return (grad_x, grad_up, grad_down, grad_bias, grad_table)
 

time: 516 us -> 862 us (1.67); the launches traced: 516 us -> 853 us
  waiting for transfers between devices: 372 us -> 686 us
  other arithmetic: 22.6 us -> 34.9 us
    ppermute x0 -> x3, waiting for transfers between devices: none -> 255 us  [doubling_sum(): lax.ppermute(summed, axis, [(i, i ^ far) for i in range(peers)])]
    psum x1, waiting for transfers between devices: 188 us -> 268 us  [per_device(): lax.psum(jnp.stack([shift_part, scale_part, gate_part], 1), 'hidden')]
    all_gather x1, waiting for transfers between devices: 21.8 us -> 0.02 us  [per_device(): hidden_act = lax.all_gather(act_share, 'width', axis=0, tiled=True)]
    add x0 -> x2, other arithmetic: none -> 10.9 us  [doubling_sum(): summed + lax.ppermute(summed, axis, [(i, i ^ far) for i in range(peers)])]
  transfers between devices with their start and end apart: 5 -> 8, of which waited for: 5 -> 6; matrix products, arithmetic and copies ran while one was open for 9% -> 8% of each run, Pallas kernels for 0% -> 0%
where the time goes in v1:
time: 862 us; the launch traced here: 853 us
  waiting for transfers between devices  686 us (80%)
  matrix products  82.9 us (10%)
  other arithmetic  34.9 us (4%)
  blocking collectives  23.6 us (3%)
  between operations  14.2 us (2%)
    psum x1, waiting for transfers between devices, per_device(): lax.psum(jnp.stack([shift_part, scale_part, gate_part], 1), 'hidden')  268 us
    ppermute x3, waiting for transfers between devices, doubling_sum(): lax.ppermute(summed, axis, [(i, i ^ far) for i in range(peers)])  255 us
    reduce_scatter x1, waiting for transfers between devices, per_device(): lax.psum_scatter(down_part, 'width', scatter_dimension=0, tiled=True)  73.8 us
    reduce_scatter x1, waiting for transfers between devices, per_device(): lax.psum_scatter(up_part, 'width', scatter_dimension=0, tiled=True)  54.3 us
    all_gather x1, waiting for transfers between devices, per_device(): lax.all_gather(pre_grad.astype(jnp.bfloat16), 'width', axis=0, tiled=True)  34.2 us
  transfers between devices with their start and end apart: 8, of which 6 were waited for; matrix products, arithmetic and copies ran while one was open for 8% of the time, Pallas kernels for 0%

profile of v1, /device:TPU:0, one launch (start us, length us, event | category | flops | bytes accessed | tf_op | source)
XLA Modules:
  0.0 853.0 jit_solution(11700602227299730101)
XLA Ops:
  7.2 0.0 copy-start
  7.2 0.0 copy-start.2
  7.2 0.0 copy-start.9
  7.2 0.0 reduce-scatter.5.cloned.1.call-start
  7.3 2.9 fusion.3
  10.1 12.7 %all-reduce.1 = (f32[1152]{0:T(1024)S(1)}, f32[1152]{0:T(1024)S(1)}) all-reduce(f32[1152]{0:T(1024)S(1)} %get-tuple-element.8, f32[1152]{0:T(1024)S(1)} %get-tuple-element.7), channel_id=1, replica_groups=mesh['width'=4,'hidden'=8] {'width'}, use_global_device_ids=true, to_apply=%region_3.0 | all-reduce | flops 2304 | bytes 18432 | tf_op jit(solution)/shard_map/psum | solution.py:44
  22.9 0.0 copy-done
  22.9 1.0 fusion.34
  23.9 0.0 copy-start.8
  23.9 0.0 slice-start
  23.9 3.4 convolution_add_fusion.1
  27.2 0.0 copy-start.3
  27.2 0.0 copy-done.8
  27.3 2.5 copy-done.3
  29.8 0.0 copy-done.2
  29.8 0.0 copy-done.9
  29.8 3.7 fusion.1
  33.5 0.0 copy-start.5
  33.5 1.6 copy-done.5
  35.1 0.0 slice-done
  35.1 0.0 slice-done.1
  35.1 7.7 fusion.42
  42.9 0.0 reduce-scatter.5.cloned.1.call-update
  42.9 0.0 reduce-scatter.3.cloned.1.call-start
  42.9 4.5 fusion
  47.4 1.7 copy-done.6
  49.1 10.2 %fusion.41 = f32[1152,1728]{1,0:T(8,128)} fusion(bf16[1152,1280]{1,0:T(8,128)(2,1)S(1)} %fusion, bf16[1728,1280]{1,0:T(8,128)(2,1)} %param.12), kind=kOutput, calls=%fused_computation.59 | convolution fusion | flops 5096079360 | bytes 15335424 | tf_op jit(solution)/shard_map/dot_general | solution.py:58
  59.3 0.0 reduce-scatter.3.cloned.1.call-update
  59.3 0.3 all-gather.3.cloned.1.call-start
  59.6 54.3 %reduce-scatter.5.cloned.1.call-done = f32[288,1728]{1,0:T(8,128)} async-done(((f32[1152,1728]{1,0:T(8,128)}), f32[288,1728]{1,0:T(8,128)}) %reduce-scatter.5.cloned.1.call-update) | async-done | bytes 1990672 | tf_op jit(solution)/shard_map/reduce_scatter | solution.py:52
  113.9 73.8 %reduce-scatter.3.cloned.1.call-done = f32[288,1728]{1,0:T(8,128)} async-done(((f32[1152,1728]{1,0:T(8,128)}), f32[288,1728]{1,0:T(8,128)}) %reduce-scatter.3.cloned.1.call-update) | async-done | bytes 1990672 | tf_op jit(solution)/shard_map/reduce_scatter | solution.py:59
  187.8 5.1 fusion.39
  192.9 0.0 all-gather.3.cloned.1.call-update
  192.9 0.0 all-gather.5.cloned.1.call-start
  193.0 34.2 %all-gather.3.cloned.1.call-done = bf16[1152,1728]{1,0:T(8,128)(2,1)} async-done(((bf16[288,1728]{1,0:T(8,128)(2,1)}), bf16[1152,1728]{1,0:T(8,128)(2,1)}) %all-gather.3.cloned.1.call-update) | async-done | bytes 3981328 | tf_op jit(solution)/shard_map/all_gather | solution.py:63
  227.2 8.6 %fusion.43 = f32[1152,1280]{1,0:T(8,128)S(1)} fusion(bf16[1152,1728]{1,0:T(8,128)(2,1)} %all-gather.3.cloned.1.call-done, bf16[1280,1728]{0,1:T(8,128)(2,1)} %param.10), kind=kOutput, calls=%fused_computation.61 | convolution fusion | flops 5096079360 | bytes 14303232 | tf_op jit(solution)/shard_map/dot_general | solution.py:66
  235.8 0.0 copy-start.4
  235.8 1.5 collective-permute-start
  237.3 127.8 %collective-permute-done = f32[1152,1280]{1,0:T(8,128)S(1)} collective-permute-done((f32[1152,1280]{1,0:T(8,128)S(1)}, f32[1152,1280]{1,0:T(8,128)S(1)}, u32[]{:S(2)}, u32[]{:S(2)}) %collective-permute-start) | collective-permute-done | bytes 5898272 | tf_op jit(solution)/shard_map/ppermute | solution.py:13
  365.1 3.3 add.69
  368.4 0.0 copy-done.4
  368.4 1.5 collective-permute-start.1
  369.8 0.0 all-gather.5.cloned.1.call-update
  369.9 0.0 all-reduce.4.cloned.1.call-start
  369.9 127.1 %collective-permute-done.1 = f32[1152,1280]{1,0:T(8,128)} collective-permute-done((f32[1152,1280]{1,0:T(8,128)}, f32[1152,1280]{1,0:T(8,128)}, u32[]{:S(2)}, u32[]{:S(2)}) %collective-permute-start.1) | collective-permute-done | bytes 5898272 | tf_op jit(solution)/shard_map/ppermute | solution.py:13
  497.0 7.6 add.70
  504.7 2.4 collective-permute-start.2
  507.1 4.7 convolution_bitcast_fusion.1
  511.8 0.0 all-gather.5.cloned.1.call-done
  511.9 9.5 %convolution_multiply_fusion = f32[1152,1280]{1,0:T(8,128)S(1)} fusion(bf16[1152,1728]{1,0:T(8,128)(2,1)} %all-gather.5.cloned.1.call-done, bf16[1728,1280]{1,0:T(8,128)(2,1)} %param.12, bf16[1152,1280]{1,0:T(8,128)(2,1)} %param.9), kind=kOutput, calls=%fused_computation | convolution fusion | flops 5099028480 | bytes 17252352 | tf_op jit(solution)/shard_map/dot_general | solution.py:55
  521.4 2.1 convolution_bitcast_fusion
  523.5 5.5 fusion.16
  529.0 0.7 pad_maximum_fusion
  529.7 0.0 all-reduce.4.cloned.1.call-update
  529.7 0.0 copy-start.7
  529.7 0.0 copy-start.12
  529.8 11.0 %fusion.44 = f32[1280,1728]{0,1:T(8,128)} fusion(bf16[1152,1280]{1,0:T(8,128)(2,1)} %copy-done.5, bf16[1152,1728]{1,0:T(8,128)(2,1)} %all-gather.3.cloned.1.call-done), kind=kOutput, calls=%fused_computation.62 | convolution fusion | flops 5096079360 | bytes 15777792 | tf_op jit(solution)/shard_map/dot_general | solution.py:65
  540.8 8.7 %fusion.45 = f32[1728,1280]{1,0:T(8,128)} fusion(bf16[1152,1728]{1,0:T(8,128)(2,1)S(1)} %copy-done.12, bf16[1152,1280]{1,0:T(8,128)(2,1)S(1)} %copy-done.7), kind=kOutput, calls=%fused_computation.63 | convolution fusion | flops 5096079360 | bytes 15777792 | tf_op jit(solution)/shard_map/dot_general | solution.py:64
  549.6 268.4 %all-reduce.4.cloned.1.call-done = f32[16,3,1280]{2,0,1:T(8,128)} async-done(((f32[16,3,1280]{2,0,1:T(8,128)}), f32[16,3,1280]{2,0,1:T(8,128)}) %all-reduce.4.cloned.1.call-update) | async-done | bytes 245776 | tf_op jit(solution)/shard_map/psum | solution.py:69
  818.0 2.2 fusion.32
  820.2 0.0 collective-permute-done.2
  820.2 9.4 %fusion.38 = (f32[1152]{0:T(1024)S(1)}, f32[1152]{0:T(1024)S(1)}, f32[1152,1280]{1,0:T(8,128)}) fusion(f32[1152]{0:T(1024)S(1)} %get-tuple-element.19, f32[1152]{0:T(1024)S(1)} %get-tuple-element.18, bf16[1152,1280]{1,0:T(8,128)(2,1)S(1)} %copy-done.2, f32[1152,1280]{1,0:T(8,128)} %copy-done.3, f32[1152,1280]{1,0:T(8,128)} %add.70, ...), kind=kLoop, calls=%fused_computation.57 | loop fusion | flops 11794176 | bytes 26560512 | tf_op jit(solution)/shard_map/reduce_sum | solution.py:24
  829.6 10.8 %all-reduce = (f32[1152]{0:T(1024)S(1)}, f32[1152]{0:T(1024)S(1)}, f32[1728]{0:T(1024)}) all-reduce(f32[1152]{0:T(1024)S(1)} %get-tuple-element.6, f32[1152]{0:T(1024)S(1)} %get-tuple-element.5, f32[1728]{0:T(1024)S(1)} %get-tuple-element.14), channel_id=1, replica_groups=mesh['width'=4,'hidden'=8] {'width'}, use_global_device_ids=true, to_apply=%region_9.0 | all-reduce | flops 4032 | bytes 32256 | tf_op jit(solution)/shard_map/psum | solution.py:24
  840.4 5.9 fusion.2
  (13 shorter events, 0.0 us)
Async XLA Ops:
  7.2 15.7 %copy-start = (f32[32,3,1280]{2,0,1:T(8,128)S(1)}, f32[32,3,1280]{2,0,1:T(8,128)}, u32[]{:S(2)}) copy-start(f32[32,3,1280]{2,0,1:T(8,128)} %param.13) | copy-start | bytes 1474564
  7.2 22.6 %copy-start.2 = (bf16[1152,1280]{1,0:T(8,128)(2,1)S(1)}, bf16[1152,1280]{1,0:T(8,128)(2,1)}, u32[]{:S(2)}) copy-start(bf16[1152,1280]{1,0:T(8,128)(2,1)} %param.8) | copy-start | bytes 8847364
  7.2 22.6 %copy-start.9 = (s32[1152]{0:T(1024)S(1)}, s32[1152]{0:T(1024)}, u32[]{:S(2)}) copy-start(s32[1152]{0:T(1024)} %param.14) | copy-start | bytes 13828
  7.2 106.7 %reduce-scatter.5.cloned.1.call-start = ((), (), s32[]{:S(2)}) async-start(), calls=%async_computation.3 | async-start | bytes 10321920 | tf_op jit(solution)/shard_map/reduce_scatter | solution.py:52
  23.9 3.4 copy-start.8
  23.9 11.3 %slice-start = ((s8[4423680]{0:T(1024)(128)(4,1)}), s8[4194304]{0:T(1024)(128)(4,1)S(1)}, s32[]{:S(2)}) async-start(s8[4423680]{0:T(1024)(128)(4,1)} %bitcast.35), calls=%async_computation.7 | async-start | bytes 8388608
  27.2 2.5 copy-start.3
  29.8 5.4 slice-start.1
  33.5 1.6 copy-start.5
  42.9 144.9 %reduce-scatter.3.cloned.1.call-start = ((), (), s32[]{:S(2)}) async-start(), calls=%async_computation.2 | async-start | bytes 10321920 | tf_op jit(solution)/shard_map/reduce_scatter | solution.py:59
  47.4 1.7 copy-start.6
  59.3 128.5 %copy-start.10 = (f32[1728]{0:T(1024)S(1)}, f32[1728]{0:T(1024)}, u32[]{:S(2)}) copy-start(f32[1728]{0:T(1024)} %param.11) | copy-start | bytes 20740
  59.3 167.8 %all-gather.3.cloned.1.call-start = ((), (), s32[]{:S(2)}) async-start(), calls=%async_computation.4 | async-start | bytes 5160960 | tf_op jit(solution)/shard_map/all_gather | solution.py:63
  192.9 318.9 %all-gather.5.cloned.1.call-start = ((), (), s32[]{:S(2)}) async-start(), calls=%async_computation.5 | async-start | bytes 5160960 | tf_op jit(solution)/shard_map/all_gather | solution.py:54
  235.8 132.6 %copy-start.4 = (f32[1152,1280]{1,0:T(8,128)}, f32[1152,1280]{1,0:T(8,128)S(1)}, u32[]{:S(2)}) copy-start(f32[1152,1280]{1,0:T(8,128)S(1)} %fusion.43) | copy-start | bytes 17694724
  235.8 129.3 %collective-permute-start = (f32[1152,1280]{1,0:T(8,128)S(1)}, f32[1152,1280]{1,0:T(8,128)S(1)}, u32[]{:S(2)}, u32[]{:S(2)}) collective-permute-start(f32[1152,1280]{1,0:T(8,128)S(1)} %fusion.43), channel_id=1, source_target_pairs={{0,1},{1,0},{2,3},{3,2},{4,5},{5,4},{6,7},{7,6},{8,9},{9,8},{10,11... | collective-permute-start | bytes 17694728 | tf_op jit(solution)/shard_map/ppermute | solution.py:13
  368.4 128.7 %collective-permute-start.1 = (f32[1152,1280]{1,0:T(8,128)}, f32[1152,1280]{1,0:T(8,128)}, u32[]{:S(2)}, u32[]{:S(2)}) collective-permute-start(f32[1152,1280]{1,0:T(8,128)} %add.69), channel_id=1, source_target_pairs={{0,2},{1,3},{2,0},{3,1},{4,6},{5,7},{6,4},{7,5},{8,10},{9,11},{10,... | collective-permute-start | bytes 17694728 | tf_op jit(solution)/shard_map/ppermute | solution.py:13
  369.9 448.1 %all-reduce.4.cloned.1.call-start = ((), (), s32[]{:S(2)}) async-start(), calls=%async_computation.6 | async-start | bytes 491520 | tf_op jit(solution)/shard_map/psum | solution.py:69
  504.7 315.5 %collective-permute-start.2 = (f32[1152,1280]{1,0:T(8,128)}, f32[1152,1280]{1,0:T(8,128)}, u32[]{:S(2)}, u32[]{:S(2)}) collective-permute-start(f32[1152,1280]{1,0:T(8,128)} %add.70), channel_id=1, source_target_pairs={{0,4},{1,5},{2,6},{3,7},{4,0},{5,1},{6,2},{7,3},{8,12},{9,13},{10,... | collective-permute-start | bytes 17694728 | tf_op jit(solution)/shard_map/ppermute | solution.py:13
  529.7 11.1 %copy-start.7 = (bf16[1152,1280]{1,0:T(8,128)(2,1)S(1)}, bf16[1152,1280]{1,0:T(8,128)(2,1)}, u32[]{:S(2)}) copy-start(bf16[1152,1280]{1,0:T(8,128)(2,1)} %copy-done.6) | copy-start | bytes 8847364
  529.7 11.1 %copy-start.12 = (bf16[1152,1728]{1,0:T(8,128)(2,1)S(1)}, bf16[1152,1728]{1,0:T(8,128)(2,1)}, u32[]{:S(2)}) copy-start(bf16[1152,1728]{1,0:T(8,128)(2,1)} %all-gather.5.cloned.1.call-done) | copy-start | bytes 11943940
  540.8 277.2 %copy-start.11 = (s32[16]{0:T(128)S(1)}, s32[16]{0:T(128)}, u32[]{:S(2)}) copy-start(s32[16]{0:T(128)} %param.15) | copy-start | bytes 196
  840.4 5.9 copy-start.1
Sparse Core Ops, SparseCore 0:
  43.0 70.8 reduce-scatter.4
  117.2 70.5 reduce-scatter.2
  193.1 34.0 all-gather.2
  370.0 33.1 all-gather.4
  529.9 288.0 all-reduce.3
